TPU v7x, 512 devices: a whole 4x8x8 slice. The times are simulated.
512 devices in a mesh: pair: 64 (over y, z), intg: 8 (over x, core).
Axes of the slice: x: 4, y: 8, z: 8, core: 2. Of those that a mesh axis runs over, the one named last changes fastest.
Arguments:
- amplitudes: bfloat16 [512, 128, 1024], P('pair'), may hold values from -6 to 6
- integrals: bfloat16 [2048, 128, 1024], P('intg', 'pair'), may hold values from -0.015625 to 0.015625
- tile_irreps: int32 [24], replicated, may hold values from 0 to 1
- screening: int32 [128], replicated, may hold values 0 or 1
- slot_tiles: int32 [128], replicated, may hold values from 0 to 127, each once
- pair_list: int32 [512, 2], P('pair'), may hold values from 0 to 299
- occupied_energy: float32 [300], replicated, may hold values from -1.2 to -0.3
- virtual_energy: float32 [768], replicated, may hold values from 0.2 to 1.5
Outputs:
- update: float32 [512, 2048], P('pair', 'intg')
Inputs may be any that keep to these rules, and one draw needn't show every extreme that they name: slot_tiles names every cd tile pair of the slab exactly once.
All inputs are finite; a program needn't handle non-finite values.
Results may differ from a plain program's by a relative error of at most 0.0003.
Values may be sent and summed in bfloat16 or wider, within the bound.
No kernel may reach another device: no remote copies, remote signals or barrier semaphores. Data moves between devices by JAX's collectives and lax.ppermute only.
A program may use at most 64 MiB of HBM per device.

v0:
```python
import jax
import jax.numpy as jnp
from jax import lax
from jax.sharding import PartitionSpec as P

TILE = 32
NT = 24


def lookup(table, index):
    places = jnp.arange(table.shape[0], dtype=jnp.int32)
    return jnp.sum(jnp.where(places[None, :] == index[:, None], table[None, :], 0), axis=1)


def on_device(
    amplitudes,
    integrals,
    tile_irreps,
    screening,
    slot_tiles,
    pair_list,
    occupied_energy,
    virtual_energy,
):
    slots_here = integrals.shape[1]
    ab_rows = integrals.shape[0]
    block = lax.axis_index("intg")
    owner = lax.axis_index("pair")
    first_tile = block // NT
    second_tile = block % NT
    sym_ab = jnp.bitwise_xor(
        lookup(tile_irreps, first_tile[None]), lookup(tile_irreps, second_tile[None])
    )
    my_slots = lax.dynamic_slice_in_dim(slot_tiles, owner * slots_here, slots_here)
    sym_cd = jnp.bitwise_xor(
        lookup(tile_irreps, my_slots // NT), lookup(tile_irreps, my_slots % NT)
    )
    keep = jnp.where(sym_cd == sym_ab, 1.0, 0.0).astype(jnp.float32) * lookup(
        screening, my_slots
    ).astype(jnp.float32)
    ordered = jnp.take(amplitudes, slot_tiles, axis=1)
    columns = lax.all_to_all(ordered, "pair", split_axis=1, concat_axis=0, tiled=True)
    masked_ints = integrals * keep.astype(jnp.bfloat16)[None, :, None]
    ladder = lax.psum_scatter(
        lax.dot_general(
            columns, masked_ints, (((1, 2), (1, 2)), ((), ())), preferred_element_type=jnp.float32
        ),
        "pair",
        scatter_dimension=0,
        tiled=True,
    )
    occupied_sum = lookup(occupied_energy, pair_list[:, 0]) + lookup(
        occupied_energy, pair_list[:, 1]
    )
    first_energy = lax.dynamic_slice_in_dim(virtual_energy, first_tile * TILE, TILE)
    second_energy = lax.dynamic_slice_in_dim(virtual_energy, second_tile * TILE, TILE)
    virtual_sum = jnp.repeat(first_energy[: ab_rows // TILE], TILE) + jnp.tile(
        second_energy, ab_rows // TILE
    )
    denom = occupied_sum[:, None] - virtual_sum[None, :]
    return ladder / denom


def solution(mesh):
    placed = (
        P("pair", None, None),
        P("intg", "pair", None),
        P(),
        P(),
        P(),
        P("pair", None),
        P(),
        P(),
    )
    return jax.shard_map(
        on_device, mesh=mesh, in_specs=placed, out_specs=P("pair", "intg"), check_vma=False
    )
```

profile of v0, /device:TPU:2, one launch (start us, length us, event | category | flops | bytes accessed | tf_op | source)
XLA Modules:
  0.0 256.4 jit_solution(17313821855280942886)
XLA Ops:
  6.5 0.8 compare_select_fusion
  7.3 0.7 compare_and_fusion
  8.0 0.1 copy-done
  8.1 8.1 %gather_fusion = bf16[128,8,1024]{2,0,1:T(8,128)(2,1)} fusion(bf16[8,128,1024]{2,1,0:T(8,128)(2,1)S(1)} %copy-done, s32[1024]{0:T(1024)S(1)} %pad_clamp_fusion), kind=kCustom, calls=%fused_computation | custom fusion | bytes 4194816 | tf_op jit(solution)/shard_map/jit(_take)/gather | solution.py:41
  16.2 1.8 select_bitcast_fusion
  18.0 2.4 copy.16
  20.5 17.0 %all-to-all-start = ((bf16[8,128,1024]{2,0,1:T(8,128)(2,1)}), bf16[8,128,1024]{2,0,1:T(8,128)(2,1)}, u32[]{:S(2)}, u32[]{:S(2)}) async-start(bf16[8,128,1024]{2,0,1:T(8,128)(2,1)} %copy.16), calls=%async_computation | async-start | bytes 4194304 | tf_op jit(solution)/shard_map/all_to_all | solution.py:42
  37.5 0.0 all-reduce.3.cloned.1.call-start
  37.6 0.6 fusion.11
  39.5 0.1 and_select_fusion.1
  39.6 0.8 fusion.14
  40.5 0.2 fusion.9
  40.7 0.2 fusion.8
  40.9 1.9 broadcast_multiply_fusion
  42.9 46.4 %all-to-all-done = bf16[8,128,1024]{2,0,1:T(8,128)(2,1)} async-done(((bf16[8,128,1024]{2,0,1:T(8,128)(2,1)}), bf16[8,128,1024]{2,0,1:T(8,128)(2,1)}, u32[]{:S(2)}, u32[]{:S(2)}) %all-to-all-start) | async-done | bytes 2097184 | tf_op jit(solution)/shard_map/all_to_all | solution.py:42
  89.3 3.4 %fusion.3 = f32[512,256]{1,0:T(8,128)} fusion(bf16[8,64,2,1024]{3,0,2,1:T(8,128)(2,1)} %bitcast.1, bf16[256,2,1024]{2,1,0:T(2,128)(2,1)} %broadcast_multiply_fusion), kind=kOutput, calls=%fused_computation.5 | convolution fusion | flops 536870912 | bytes 3670016 | tf_op jit(solution)/shard_map/dot_general | solution.py:45
  92.7 0.0 all-reduce.3.cloned.1.call-update
  92.7 0.1 broadcast_add_fusion
  92.8 0.1 add.57
  92.9 1.3 dynamic-slice
  94.8 0.0 copy-done.3
  94.8 0.2 select_reduce_fusion
  95.1 153.1 %all-reduce.3.cloned.1.call-done = f32[512,256]{1,0:T(8,128)} async-done(((f32[512,256]{1,0:T(8,128)}), f32[512,256]{1,0:T(8,128)}) %all-reduce.3.cloned.1.call-update) | async-done | bytes 524304
  248.2 1.4 dynamic-slice_divide_fusion
  (17 shorter events, 0.1 us)
Async XLA Ops:
  6.5 1.6 copy-start
  20.5 17.1 %copy-start.2 = (s32[24]{0:T(128)S(1)}, s32[24]{0:T(128)}, u32[]{:S(2)}) copy-start(s32[24]{0:T(128)} %param.10) | copy-start | bytes 292
  20.5 19.0 %copy-start.5 = (s32[128]{0:T(128)S(1)}, s32[128]{0:T(128)}, u32[]{:S(2)}) copy-start(s32[128]{0:T(128)} %param.12) | copy-start | bytes 1540
  20.5 20.0 %copy-start.6 = (s32[128]{0:T(128)S(1)}, s32[128]{0:T(128)}, u32[]{:S(2)}) copy-start(s32[128]{0:T(128)} %param.11) | copy-start | bytes 1540
  20.5 20.4 %copy-start.1 = (bf16[256,2,1024]{2,1,0:T(2,128)(2,1)S(1)}, bf16[256,2,1024]{2,1,0:T(2,128)(2,1)}, u32[]{:S(2)}) copy-start(bf16[256,2,1024]{2,1,0:T(2,128)(2,1)} %param.9) | copy-start | bytes 3145732
  20.5 68.8 %all-to-all-start = ((bf16[8,128,1024]{2,0,1:T(8,128)(2,1)}), bf16[8,128,1024]{2,0,1:T(8,128)(2,1)}, u32[]{:S(2)}, u32[]{:S(2)}) async-start(bf16[8,128,1024]{2,0,1:T(8,128)(2,1)} %copy.16), calls=%async_computation | async-start | bytes 4194304 | tf_op jit(solution)/shard_map/all_to_all | solution.py:42
  37.5 210.7 %all-reduce.3.cloned.1.call-start = ((), (), s32[]{:S(2)}) async-start(), calls=%async_computation.1 | async-start | bytes 1048576
  89.3 5.5 %copy-start.4 = (s32[8,2]{0,1:T(2,128)S(1)}, s32[8,2]{0,1:T(2,128)}, u32[]{:S(2)}) copy-start(s32[8,2]{0,1:T(2,128)} %param.13) | copy-start | bytes 196
  89.3 5.6 %copy-start.3 = (f32[300]{0:T(512)S(1)}, f32[300]{0:T(512)}, u32[]{:S(2)}) copy-start(f32[300]{0:T(512)} %param.14) | copy-start | bytes 3604
Sparse Core Ops, SparseCore 0:
  92.9 155.2 all-reduce.2
where the time goes:
time: 257 us; the launch traced here: 256 us
  waiting for transfers between devices  200 us (78%)
  starting transfers between devices  17 us (7%)
  between operations  15.5 us (6%)
  local copies, waits for them, and re-layouts  12.8 us (5%)
  other arithmetic  8.06 us (3%)
  matrix products  3.44 us (1%)
    unnamed x2, waiting for transfers between devices  153 us
    all_to_all x1, waiting for transfers between devices, on_device(): lax.all_to_all(ordered, 'pair', split_axis=1, concat_axis=0, tiled=True)  46.4 us
    all_to_all x1, starting transfers between devices, on_device(): lax.all_to_all(ordered, 'pair', split_axis=1, concat_axis=0, tiled=True)  17 us
    gather x1, local copies, waits for them, and re-layouts, on_device(): ordered = jnp.take(amplitudes, slot_tiles, axis=1)  8.06 us
  transfers between devices with their start and end apart: 2, of which 2 were waited for; matrix products, arithmetic and copies ran while one was open for 2% of the time, Pallas kernels for 0%

commit v1 on v0

--- a/solution.py
+++ b/solution.py
@@ -39,7 +39,10 @@
         screening, my_slots
     ).astype(jnp.float32)
     ordered = jnp.take(amplitudes, slot_tiles, axis=1)
-    columns = lax.all_to_all(ordered, "pair", split_axis=1, concat_axis=0, tiled=True)
+    columns = jnp.concatenate(
+        lax.all_to_all(jnp.stack(jnp.split(ordered, lax.axis_size("pair"), axis=1)), "pair", 0, 0),
+        axis=0,
+    )
     masked_ints = integrals * keep.astype(jnp.bfloat16)[None, :, None]
     ladder = lax.psum_scatter(
         lax.dot_general(

time: 257 us -> 295 us (1.15)
  local copies, waits for them, and re-layouts: 12.8 us -> 51 us
    unnamed x15 -> x78, local copies, waits for them, and re-layouts: 1.42 us -> 41.4 us
where the time goes in v1:
time: 295 us
  waiting for transfers between devices  200 us (68%)
  local copies, waits for them, and re-layouts  51 us (17%)
  starting transfers between devices  17 us (6%)
  between operations  15.5 us (5%)
  other arithmetic  8.06 us (3%)
  matrix products  3.41 us (1%)
    unnamed x2, waiting for transfers between devices  153 us
    all_to_all x1, waiting for transfers between devices, on_device(): lax.all_to_all(jnp.stack(jnp.split(ordered, lax.axis_size('pair'), axis=1...  46.4 us
    unnamed x78, local copies, waits for them, and re-layouts  41.4 us
    all_to_all x1, starting transfers between devices, on_device(): lax.all_to_all(jnp.stack(jnp.split(ordered, lax.axis_size('pair'), axis=1...  17 us
    gather x1, local copies, waits for them, and re-layouts, on_device(): ordered = jnp.take(amplitudes, slot_tiles, axis=1)  8.06 us
  transfers between devices with their start and end apart: 2, of which 2 were waited for; matrix products, arithmetic and copies ran while one was open for 2% of the time, Pallas kernels for 0%

profile of v1, /device:TPU:2, one launch (start us, length us, event | category | flops | bytes accessed | tf_op | source)
XLA Modules:
  0.0 294.5 jit_solution(4494192678080528583)
XLA Ops:
  6.5 0.8 compare_select_fusion
  7.3 0.7 compare_and_fusion
  8.1 8.1 %gather_fusion = bf16[128,8,1024]{2,0,1:T(8,128)(2,1)} fusion(bf16[8,128,1024]{2,1,0:T(8,128)(2,1)S(1)} %copy-done, s32[1024]{0:T(1024)S(1)} %pad_clamp_fusion), kind=kCustom, calls=%fused_computation | custom fusion | bytes 4194816 | tf_op jit(solution)/shard_map/jit(_take)/gather | solution.py:41
  16.2 1.8 select_bitcast_fusion
  18.7 0.6 constant_dynamic-update-slice_fusion.62
  21.2 0.6 constant_dynamic-update-slice_fusion.58
  22.5 0.6 constant_dynamic-update-slice_fusion.56
  23.7 0.6 constant_dynamic-update-slice_fusion.54
  26.3 0.6 constant_dynamic-update-slice_fusion.50
  27.6 0.6 constant_dynamic-update-slice_fusion.48
  32.0 0.7 constant_dynamic-update-slice_fusion.41
  36.4 0.6 constant_dynamic-update-slice_fusion.34
  44.1 0.6 constant_dynamic-update-slice_fusion.22
  51.7 0.7 constant_dynamic-update-slice_fusion.10
  53.0 0.6 constant_dynamic-update-slice_fusion.8
  58.7 17.0 %all-to-all-start = ((bf16[64,8,2,1024]{3,2,1,0:T(2,128)(2,1)}), bf16[64,8,2,1024]{3,2,1,0:T(2,128)(2,1)}, u32[]{:S(2)}, u32[]{:S(2)}) async-start(bf16[64,8,2,1024]{3,2,1,0:T(2,128)(2,1)} %constant_dynamic-update-slice_fusion), calls=%async_computation | async-start | bytes 4194304 | tf_op jit(solution)/shard_map/all_to_all | solution.py:43
  75.8 0.6 fusion.11
  77.8 0.8 fusion.14
  79.1 1.9 broadcast_multiply_fusion
  81.0 46.4 %all-to-all-done = bf16[64,8,2,1024]{3,2,1,0:T(2,128)(2,1)} async-done(((bf16[64,8,2,1024]{3,2,1,0:T(2,128)(2,1)}), bf16[64,8,2,1024]{3,2,1,0:T(2,128)(2,1)}, u32[]{:S(2)}, u32[]{:S(2)}) %all-to-all-start) | async-done | bytes 2097184 | tf_op jit(solution)/shard_map/all_to_all | solution.py:43
  127.5 3.4 %fusion.3 = f32[512,256]{1,0:T(8,128)} fusion(bf16[64,8,2,1024]{3,2,1,0:T(2,128)(2,1)} %all-to-all-done, bf16[256,2,1024]{2,1,0:T(2,128)(2,1)} %broadcast_multiply_fusion), kind=kOutput, calls=%fused_computation.5 | convolution fusion | flops 536870912 | bytes 3670016 | tf_op jit(solution)/shard_map/dot_general | solution.py:48
  131.3 1.3 dynamic-slice
  133.2 153.1 %all-reduce.3.cloned.1.call-done = f32[512,256]{1,0:T(8,128)} async-done(((f32[512,256]{1,0:T(8,128)}), f32[512,256]{1,0:T(8,128)}) %all-reduce.3.cloned.1.call-update) | async-done | bytes 524304
  286.3 1.4 dynamic-slice_divide_fusion
  (80 shorter events, 34.6 us)
Async XLA Ops:
  6.5 1.6 copy-start
  58.7 17.1 %copy-start.2 = (s32[24]{0:T(128)S(1)}, s32[24]{0:T(128)}, u32[]{:S(2)}) copy-start(s32[24]{0:T(128)} %param.10) | copy-start | bytes 292
  58.7 19.0 %copy-start.5 = (s32[128]{0:T(128)S(1)}, s32[128]{0:T(128)}, u32[]{:S(2)}) copy-start(s32[128]{0:T(128)} %param.12) | copy-start | bytes 1540
  58.7 20.0 %copy-start.6 = (s32[128]{0:T(128)S(1)}, s32[128]{0:T(128)}, u32[]{:S(2)}) copy-start(s32[128]{0:T(128)} %param.11) | copy-start | bytes 1540
  58.7 20.4 %copy-start.1 = (bf16[256,2,1024]{2,1,0:T(2,128)(2,1)S(1)}, bf16[256,2,1024]{2,1,0:T(2,128)(2,1)}, u32[]{:S(2)}) copy-start(bf16[256,2,1024]{2,1,0:T(2,128)(2,1)} %param.9) | copy-start | bytes 3145732
  58.7 68.8 %all-to-all-start = ((bf16[64,8,2,1024]{3,2,1,0:T(2,128)(2,1)}), bf16[64,8,2,1024]{3,2,1,0:T(2,128)(2,1)}, u32[]{:S(2)}, u32[]{:S(2)}) async-start(bf16[64,8,2,1024]{3,2,1,0:T(2,128)(2,1)} %constant_dynamic-update-slice_fusion), calls=%async_computation | async-start | bytes 4194304 | tf_op jit(solution)/shard_map/all_to_all | solution.py:43
  75.7 210.6 %all-reduce.3.cloned.1.call-start = ((), (), s32[]{:S(2)}) async-start(), calls=%async_computation.1 | async-start | bytes 1048576
  81.0 50.0 %copy-start.4 = (s32[8,2]{0,1:T(2,128)S(1)}, s32[8,2]{0,1:T(2,128)}, u32[]{:S(2)}) copy-start(s32[8,2]{0,1:T(2,128)} %param.13) | copy-start | bytes 196
  81.0 50.0 %copy-start.3 = (f32[300]{0:T(512)S(1)}, f32[300]{0:T(512)}, u32[]{:S(2)}) copy-start(f32[300]{0:T(512)} %param.14) | copy-start | bytes 3604
Sparse Core Ops, SparseCore 0:
  131.0 155.2 all-reduce.2
